TPU v7x, 32 devices: a whole 2x2x4 slice. The times are simulated.
32 devices in a mesh: member: 8 (over y, x, core), band: 4 (over z).
Axes of the slice: x: 2, y: 2, z: 4, core: 2. Of those that a mesh axis runs over, the one named last changes fastest.
Arguments:
- controls: float32 [16, 16, 256, 512], P('member', None, 'band'), may hold values from -6 to 6
- members: float32 [16, 16, 256, 512], P('member', None, 'band'), may hold values from -6 to 6
- loc_lon: float32 [512, 512], replicated, may hold values from -0.25 to 0.25
- loc_lat: float32 [256, 256], replicated, may hold values from -0.375 to 0.375
- balance: float32 [5, 1024, 2048], P(None, 'band', 'member'), may hold values from -1 to 1
- innovation: float32 [16, 1024, 2048], P(None, 'band', 'member'), may hold values from -6 to 6
- obs_weight: float32 [16, 1024, 2048], P(None, 'band', 'member'), may hold values from 0.2 to 5
Outputs:
- gradient: float32 [16, 16, 256, 512], P('member', None, 'band')
All inputs are finite; a program needn't handle non-finite values.
Results may differ from a plain program's by a relative error of at most 0.00012.
Values sent between devices are 32-bit elements; how exact they have to be, the bound alone decides.
No kernel may reach another device: no remote copies, remote signals or barrier semaphores. Data moves between devices by JAX's collectives and lax.ppermute only.
A program may use at most 128 MiB of HBM per device.

v0:
```python
import math
import jax
import jax.numpy as jnp
from jax import lax
from jax.sharding import PartitionSpec as P

phase_fraction = (0.625, 0.875, 0.125, 0.375)
phase_start = (0, 0, 1, 1)


def with_halo(value, sides, width, wrap):
    for axis, dim in sides:
        size, length = (lax.axis_size(axis), value.shape[dim])
        up = [(i, (i + 1) % size) for i in range(size if wrap else size - 1)]
        down = [(j, i) for i, j in up]
        last = lax.slice_in_dim(value, length - width, length, axis=dim)
        leading = lax.slice_in_dim(value, 0, width, axis=dim)
        before = lax.ppermute(last, axis, up)
        after = lax.ppermute(leading, axis, down)
        value = jnp.concatenate([before, value, after], axis=dim)
    return value


def passed_along(value, axis, by):
    length = lax.axis_size(axis)
    return lax.ppermute(value, axis, [(i, (i + by) % length) for i in range(length)])


def from_behind(value, axis, steps):
    count = lax.axis_size(axis)
    leading, last = (max(0, -steps), min(count, count - steps))
    return lax.ppermute(value, axis, [(source, source + steps) for source in range(leading, last)])


def cubic_weights(fraction):
    return (
        (-(fraction**3) + 2 * fraction**2 - fraction) / 2,
        (3 * fraction**3 - 5 * fraction**2 + 2) / 2,
        (-3 * fraction**3 + 4 * fraction**2 + fraction) / 2,
        (fraction**3 - fraction**2) / 2,
    )


def refine(padded, dim_index):
    length = padded.shape[dim_index] - 4
    phase_rows = []
    for phase_index in range(4):
        weights = cubic_weights(phase_fraction[phase_index])
        summed = jnp.zeros_like(lax.slice_in_dim(padded, 0, length, axis=dim_index))
        for tap_index in range(4):
            first = phase_start[phase_index] + tap_index
            summed = summed + weights[tap_index] * lax.slice_in_dim(
                padded, first, first + length, axis=dim_index
            )
        phase_rows.append(summed)
    stacked = jnp.stack(phase_rows, axis=dim_index + 1)
    new_shape = list(padded.shape)
    new_shape[dim_index] = 4 * length
    return stacked.reshape(new_shape)


def refine_both(padded):
    return refine(refine(padded, 1), 2)


def body(controls, members, loc_lon, loc_lat, balance, innovation, obs_weight):
    highest = lax.Precision.HIGHEST
    member_scale = 1.0 / math.sqrt(controls.shape[0] * lax.axis_size("member") - 1)
    full_lon = loc_lon.shape[0]
    stripe_width = full_lon // lax.axis_size("member")
    level_ctrl, level_members = (
        lax.all_to_all(controls, "band", split_axis=1, concat_axis=2, tiled=True),
        lax.all_to_all(members, "band", split_axis=1, concat_axis=2, tiled=True),
    )
    rowwise = jnp.einsum("klyx,ux->klyu", level_ctrl, loc_lon, precision=highest)
    fields = jnp.einsum("vy,klyx->klvx", loc_lat, rowwise, precision=highest)
    partial_value = jnp.sum(level_members * fields, axis=0) * member_scale
    summed = lax.psum(partial_value, "member")
    summed = lax.all_to_all(summed, "band", split_axis=1, concat_axis=0, tiled=True)
    wrapped = jnp.concatenate([summed[:, :, -2:], summed, summed[:, :, :2]], axis=2)
    extended = lax.dynamic_slice_in_dim(
        wrapped, lax.axis_index("member") * stripe_width, stripe_width + 4, 2
    )
    padded = with_halo(extended, (("band", 1),), 2, False)
    fine_field = refine_both(padded)
    grown_field = with_halo(fine_field, (("member", 2),), 1, True)
    grown_field = with_halo(grown_field, (("band", 1),), 1, False)
    balanced = (
        balance[0] * fine_field
        + balance[1] * grown_field[:, 1:-1, 2:]
        + balance[2] * grown_field[:, 1:-1, :-2]
        + balance[3] * grown_field[:, 2:, 1:-1]
        + balance[4] * grown_field[:, :-2, 1:-1]
    )
    weighted_misfit = obs_weight * (balanced - innovation)
    pieces = balance[1:, None] * weighted_misfit[None]
    spread = with_halo(pieces, (("member", 3),), 1, True)
    spread = with_halo(spread, (("band", 2),), 1, False)
    fine_grad = (
        balance[0] * weighted_misfit
        + spread[0][:, 1:-1, :-2]
        + spread[1][:, 1:-1, 2:]
        + spread[2][:, :-2, 1:-1]
        + spread[3][:, 2:, 1:-1]
    )
    unused, pullback = jax.vjp(refine_both, padded)
    coarse_ext = pullback(fine_grad)[0]
    west_rim = passed_along(coarse_ext[:, :, :2], "member", -1)
    east_rim = passed_along(coarse_ext[:, :, -2:], "member", 1)
    core_sum = coarse_ext[:, :, 2:-2]
    core_sum = core_sum.at[:, :, -2:].add(west_rim)
    core_sum = core_sum.at[:, :, :2].add(east_rim)
    south_rim = from_behind(core_sum[:, :2], "band", -1)
    north_rim = from_behind(core_sum[:, -2:], "band", 1)
    coarse_grad = core_sum[:, 2:-2]
    coarse_grad = coarse_grad.at[:, -2:].add(south_rim)
    coarse_grad = coarse_grad.at[:, :2].add(north_rim)
    level_grad = lax.all_to_all(coarse_grad, "band", split_axis=0, concat_axis=1, tiled=True)
    weighted = (
        level_members
        * lax.all_gather(level_grad, "member", axis=2, tiled=True)[None]
        * member_scale
    )
    adjoint = jnp.einsum("klyu,ux->klyx", weighted, loc_lon, precision=highest)
    adjoint = jnp.einsum("vy,klvx->klyx", loc_lat, adjoint, precision=highest)
    adjoint = lax.all_to_all(adjoint, "band", split_axis=2, concat_axis=1, tiled=True)
    return controls + adjoint


def solution(mesh):
    return jax.shard_map(
        body,
        mesh=mesh,
        in_specs=(
            P("member", None, "band", None),
            P("member", None, "band", None),
            P(),
            P(),
            P(None, "band", "member"),
            P(None, "band", "member"),
            P(None, "band", "member"),
        ),
        out_specs=P("member", None, "band", None),
        check_vma=False,
    )
```

profile of v0, /device:TPU:0, one launch (start us, length us, event | category | flops | bytes accessed | tf_op | source)
XLA Modules:
  0.0 769.8 jit_solution(10708017313778358526)
XLA Ops:
  6.5 5.0 copy.99
  11.5 6.3 all-to-all-start
  17.9 4.9 copy.103
  22.8 88.5 %all-to-all-done = f32[2,16,64,512]{3,2,0,1:T(8,128)} async-done(((f32[2,16,64,512]{3,2,0,1:T(8,128)}), f32[2,16,64,512]{3,2,0,1:T(8,128)}, u32[]{:S(2)}, u32[]{:S(2)}) %all-to-all-start) | async-done | bytes 4194336 | tf_op jit(solution)/shard_map/all_to_all | solution.py:73
  111.3 4.9 all-to-all-start.1
  116.2 4.9 copy.101
  121.1 5.3 copy.107
  126.4 82.4 %all-to-all-done.1 = f32[2,16,64,512]{3,2,0,1:T(8,128)} async-done(((f32[2,16,64,512]{3,2,0,1:T(8,128)}), f32[2,16,64,512]{3,2,0,1:T(8,128)}, u32[]{:S(2)}, u32[]{:S(2)}) %all-to-all-start.1) | async-done | bytes 4194336 | tf_op jit(solution)/shard_map/all_to_all | solution.py:72
  208.8 2.8 copy.105
  211.6 7.2 fusion.20
  218.8 4.1 fusion.10
  222.8 1.5 broadcast_multiply_fusion.1
  224.4 61.1 %all-reduce.34.cloned.1.call-done = f32[4,256,512]{1,2,0:T(8,128)} async-done(((f32[4,256,512]{1,2,0:T(8,128)}), f32[4,256,512]{1,2,0:T(8,128)}) %all-reduce.34.cloned.1.call-update) | async-done | bytes 2097168 | tf_op jit(solution)/shard_map/psum | solution.py:78
  285.5 3.1 copy.108
  288.6 4.5 all-to-all-start.2
  293.3 46.9 %all-to-all-done.2 = f32[4,256,512]{2,0,1:T(4,128)S(1)} async-done(((f32[4,256,512]{2,0,1:T(4,128)}), f32[4,256,512]{2,0,1:T(4,128)S(1)}, u32[]{:S(2)}, u32[]{:S(2)}) %all-to-all-start.2) | async-done | bytes 2097184 | tf_op jit(solution)/shard_map/all_to_all | solution.py:79
  344.6 4.2 collective-permute-done.1
  351.1 2.3 add_bitcast_fusion.3
  353.4 3.7 pad_maximum_fusion.2
  357.1 8.6 %copy.114 = f32[16,256,64,4]{1,0,3,2:T(8,128)} copy(f32[16,256,64,4]{2,0,1,3:T(8,128)} %pad_maximum_fusion.2) | data formatting | bytes 8388608 | tf_op jit(solution)/shard_map/stack | solution.py:56
  367.9 2.6 collective-permute-done.3
  370.5 2.6 pad_maximum_fusion.3
  373.2 2.1 fusion.41
  375.3 2.6 copy.118
  380.3 5.0 collective-permute-start.5
  390.3 5.5 copy.123
  395.8 5.6 copy.124
  402.6 1.4 copy.119
  404.0 2.6 copy.122
  406.6 20.2 %fusion.3 = f32[16,256,256]{1,0,2:T(8,128)} fusion(f32[16,256,256]{1,0,2:T(8,128)} %copy.124, f32[16,256,256]{1,0,2:T(8,128)} %copy.123, f32[16,1,258]{1,0,2:T(8,128)} %copy.122, f32[16,256,1]{1,0,2:T(8,128)S(1)} %collective-permute-done.2, f32[16,256,256]{1,0,2:T(8,128)} %bitcast.240, f32[16,256,1]{1,0,2:T(8,128)S(1)} %collective-permute-done.3, ...), kind=kLoop, calls=%fused_computation.17 | loop fusion | flops 19922944 | bytes 18153728 | tf_op jit(solution)/shard_map/mul | solution.py:95
  426.8 10.8 %broadcast_multiply_fusion = f32[4,16,256,256]{2,1,3,0:T(8,128)} fusion(f32[16,256,256]{1,0,2:T(8,128)} %fusion.3, f32[4,256,256]{1,2,0:T(8,128)} %copy.125), kind=kLoop, calls=%fused_computation.3 | loop fusion | flops 4194304 | bytes 22020096 | tf_op jit(solution)/shard_map/mul | solution.py:96
  438.5 2.6 collective-permute-start.7
  441.1 2.6 collective-permute-done.6
  443.8 6.8 pad_maximum_fusion.1
  450.6 7.3 fusion.39
  457.9 6.5 copy.126
  464.4 3.1 collective-permute-start.8
  467.5 6.5 copy.127
  474.0 1.5 collective-permute-start.9
  475.5 6.4 copy.128
  481.9 6.3 copy.129
  488.2 25.8 %pad_maximum_fusion = f32[4,16,258,258]{2,1,3,0:T(8,128)} fusion(f32[4,16,1,258]{2,1,3,0:T(8,128)} %copy.129, f32[4,16,256,1]{2,1,3,0:T(8,128)S(1)} %collective-permute-done.7, f32[4,16,256,256]{2,1,3,0:T(8,128)} %broadcast_multiply_fusion, f32[4,16,256,1]{2,1,3,0:T(8,128)S(1)} %collective-permute-done.6, f32[4,16,1,258]{2,1,3,0:T(8,128)} %copy.128), kind=kLoop, calls=%fused_computation | loop fusion | flops 17040384 | bytes 34080768 | tf_op jit(solution)/shard_map/concatenate | solution.py:20
  514.1 17.6 %slice_bitcast_fusion.3 = (f32[16,258,258]{1,0,2:T(8,128)}, f32[16,258,258]{1,0,2:T(8,128)}, f32[16,258,258]{1,0,2:T(8,128)}, f32[16,258,258]{1,0,2:T(8,128)}) fusion(f32[4,16,258,258]{2,1,3,0:T(8,128)} %pad_maximum_fusion), kind=kLoop, calls=%fused_computation.7 | loop fusion | bytes 34080768 | tf_op jit(solution)/shard_map/squeeze | solution.py:101
  531.7 9.4 %slice_add_fusion = f32[16,256,256]{1,0,2:T(8,128)S(1)} fusion(f32[16,258,258]{1,0,2:T(8,128)} %get-tuple-element.56, f32[16,258,258]{1,0,2:T(8,128)} %get-tuple-element.57, f32[16,258,258]{1,0,2:T(8,128)} %get-tuple-element.58, f32[16,258,258]{1,0,2:T(8,128)} %get-tuple-element.55, f32[16,256,256]{1,0,2:T(8,128)S(1)} %copy-done.1, f32[256,256]{0,1:T(8,128)S(1)} %copy.102), kind=kLoop, calls=%fused_computation.9 | loop fusion | flops 5242880 | bytes 25427968 | tf_op jit(solution)/shard_map/add | solution.py:100
  541.1 3.0 fusion.17
  544.2 1.6 multiply_bitcast_fusion.9
  545.7 5.0 pad_add_fusion
  550.7 2.2 copy.139
  554.8 1.7 collective-permute-start.10
  558.5 15.6 %scatter-add.14 = f32[16,68,64]{2,0,1:T(8,128)S(1)} dynamic-update-slice(f32[16,68,64]{2,0,1:T(8,128)S(1)} %slice.339, f32[16,68,2]{2,0,1:T(8,128)S(1)} %slice_add_fusion.4, s32[]{:T(128)} %constant.132.clone.1, s32[]{:T(128)} %constant.132.clone.1, s32[]{:T(128)} %constant.145.clone.1) | dynamic-update-slice | bytes 17412 | tf_op jit(solution)/shard_map/scatter-add | solution.py:111
  574.8 7.0 scatter-add.15
  583.2 5.2 collective-permute-start.13
  588.4 1.4 collective-permute-done.13
  590.4 13.3 %all_to_all.90 = f32[4,1,16384]{2,1,0:T(1,128)S(1)} all-to-all(f32[4,1,16384]{2,1,0:T(1,128)S(1)} %reshape.202), channel_id=1, replica_groups=mesh['member'=8,'band'=4] {'band'}, dimensions={0} | all-to-all | bytes 524288 | tf_op jit(solution)/shard_map/all_to_all | solution.py:118
  604.2 1.4 reduce.8
  607.2 27.2 %all-gather.2.cloned.1.call-done = f32[4,256,512]{1,2,0:T(8,128)} async-done(((f32[4,256,64]{1,2,0:T(8,128)}), f32[4,256,512]{1,2,0:T(8,128)}) %all-gather.2.cloned.1.call-update) | async-done | bytes 2097168 | tf_op jit(solution)/shard_map/all_gather | solution.py:121
  634.4 1.9 copy.154
  636.3 9.8 %fusion.11 = f32[2,4,256,512]{2,3,1,0:T(8,128)S(1)} fusion(f32[2,4,256,512]{3,2,1,0:T(8,128)} %bitcast.242, f32[4,256,512]{2,1,0:T(8,128)S(1)} %copy.154, f32[512,512]{1,0:T(8,128)S(1)} %copy-done), kind=kOutput, calls=%fused_computation.33 | convolution fusion | flops 6444548096 | bytes 11534336 | tf_op jit(solution)/shard_map/klyu,ux->klyx/dot_general | solution.py:124
  646.1 5.0 convolution_bitcast_fusion
  651.1 5.5 copy.156
  656.5 98.4 %all_to_all.91 = f32[2,4,256,512]{3,1,0,2:T(4,128)S(1)} all-to-all(f32[2,4,256,512]{3,1,0,2:T(4,128)} %copy.156), channel_id=1, replica_groups=mesh['member'=8,'band'=4] {'band'}, dimensions={2} | all-to-all | bytes 8388608 | tf_op jit(solution)/shard_map/all_to_all | solution.py:126
  754.9 2.4 copy.157
  758.1 1.5 copy-done.2
  759.5 3.0 add.233
  (77 shorter events, 27.9 us)
Async XLA Ops:
  6.5 205.0 %copy-start = (f32[512,512]{1,0:T(8,128)S(1)}, f32[512,512]{1,0:T(8,128)}, u32[]{:S(2)}) copy-start(f32[512,512]{1,0:T(8,128)} %param.17) | copy-start | bytes 3145732
  11.5 99.8 %all-to-all-start = ((f32[2,16,64,512]{3,2,0,1:T(8,128)}), f32[2,16,64,512]{3,2,0,1:T(8,128)}, u32[]{:S(2)}, u32[]{:S(2)}) async-start(f32[2,16,64,512]{3,2,0,1:T(8,128)} %copy.99), calls=%async_computation | async-start | bytes 8388608 | tf_op jit(solution)/shard_map/all_to_all | solution.py:73
  111.3 97.5 %all-to-all-start.1 = ((f32[2,16,64,512]{3,2,0,1:T(8,128)}), f32[2,16,64,512]{3,2,0,1:T(8,128)}, u32[]{:S(2)}, u32[]{:S(2)}) async-start(f32[2,16,64,512]{3,2,0,1:T(8,128)} %copy.103), calls=%async_computation.1 | async-start | bytes 8388608 | tf_op jit(solution)/shard_map/all_to_all | solution.py:72
  116.2 169.3 %all-reduce.34.cloned.1.call-start = ((), (), s32[]{:S(2)}) async-start(), calls=%async_computation.5 | async-start | bytes 4194304 | tf_op jit(solution)/shard_map/psum | solution.py:78
  211.5 7.2 copy-start.3
  211.5 7.2 copy-start.4
  288.6 51.6 %all-to-all-start.2 = ((f32[4,256,512]{2,0,1:T(4,128)}), f32[4,256,512]{2,0,1:T(4,128)S(1)}, u32[]{:S(2)}, u32[]{:S(2)}) async-start(f32[4,256,512]{2,0,1:T(4,128)} %copy.108), calls=%async_computation.2 | async-start | bytes 4194304 | tf_op jit(solution)/shard_map/all_to_all | solution.py:79
  293.1 341.3 %all-gather.2.cloned.1.call-start = ((), (), s32[]{:S(2)}) async-start(), calls=%async_computation.6 | async-start | bytes 2359296 | tf_op jit(solution)/shard_map/all_gather | solution.py:121
  341.8 2.7 collective-permute-start
  343.1 5.6 collective-permute-start.1
  366.5 1.4 collective-permute-start.2
  366.5 4.1 collective-permute-start.3
  377.9 24.7 %collective-permute-start.4 = (f32[16,1,258]{2,0,1:T(8,128)S(1)}, f32[16,1,258]{2,0,1:T(8,128)S(1)}, u32[]{:S(2)}, u32[]{:S(2)}) collective-permute-start(f32[16,1,258]{2,0,1:T(8,128)S(1)} %copy.118), channel_id=1, source_target_pairs={{1,0},{2,1},{3,2},{5,4},{6,5},{7,6},{9,8},{10,9},{11,10},{13,12},{... | collective-permute-start | bytes 49544 | tf_op jit(solution)/shard_map/ppermute | solution.py:19
  380.3 23.7 %collective-permute-start.5 = (f32[16,1,258]{2,0,1:T(8,128)S(1)}, f32[16,1,258]{2,0,1:T(8,128)S(1)}, u32[]{:S(2)}, u32[]{:S(2)}) collective-permute-start(f32[16,1,258]{2,0,1:T(8,128)S(1)} %copy.121), channel_id=1, source_target_pairs={{0,1},{1,2},{2,3},{4,5},{5,6},{6,7},{8,9},{9,10},{10,11},{12,13},{... | collective-permute-start | bytes 49544 | tf_op jit(solution)/shard_map/ppermute | solution.py:18
  395.7 5.6 slice-start
  438.4 5.3 collective-permute-start.6
  438.5 5.3 collective-permute-start.7
  464.4 11.1 %collective-permute-start.8 = (f32[4,16,1,258]{3,1,2,0:T(8,128)S(1)}, f32[4,16,1,258]{3,1,2,0:T(8,128)S(1)}, u32[]{:S(2)}, u32[]{:S(2)}) collective-permute-start(f32[4,16,1,258]{3,1,2,0:T(8,128)S(1)} %copy.126), channel_id=1, source_target_pairs={{0,1},{1,2},{2,3},{4,5},{5,6},{6,7},{8,9},{9,10},{10,11},{12,13},{... | collective-permute-start | bytes 198152 | tf_op jit(solution)/shard_map/ppermute | solution.py:18
  474.0 7.9 %collective-permute-start.9 = (f32[4,16,1,258]{3,1,2,0:T(8,128)S(1)}, f32[4,16,1,258]{3,1,2,0:T(8,128)S(1)}, u32[]{:S(2)}, u32[]{:S(2)}) collective-permute-start(f32[4,16,1,258]{3,1,2,0:T(8,128)S(1)} %copy.127), channel_id=1, source_target_pairs={{1,0},{2,1},{3,2},{5,4},{6,5},{7,6},{9,8},{10,9},{11,10},{13,12},{... | collective-permute-start | bytes 198152 | tf_op jit(solution)/shard_map/ppermute | solution.py:19
  514.1 17.6 %copy-start.1 = (f32[16,256,256]{1,0,2:T(8,128)S(1)}, f32[16,256,256]{1,0,2:T(8,128)}, u32[]{:S(2)}) copy-start(f32[16,256,256]{1,0,2:T(8,128)} %fusion.3) | copy-start | bytes 12582916
  554.8 3.1 collective-permute-start.10
  557.0 17.4 %collective-permute-start.11 = (f32[16,68,2]{1,0,2:T(8,128)S(1)}, f32[16,68,2]{1,0,2:T(8,128)S(1)}, u32[]{:S(2)}, u32[]{:S(2)}) collective-permute-start(f32[16,68,2]{1,0,2:T(8,128)S(1)} %copy.149), channel_id=1, source_target_pairs={{0,4},{4,8},{8,12},{12,16},{16,20},{20,24},{24,28},{28,0},{1,5},{5... | collective-permute-start | bytes 26120 | tf_op jit(solution)/shard_map/ppermute | solution.py:26
  581.9 6.5 collective-permute-start.12
  583.2 6.6 collective-permute-start.13
  636.3 9.8 %copy-start.5 = (f32[256,256]{1,0:T(8,128)S(1)}, f32[256,256]{1,0:T(8,128)}, u32[]{:S(2)}) copy-start(f32[256,256]{1,0:T(8,128)} %param.18) | copy-start | bytes 786436
  757.3 2.2 copy-start.2
Sparse Core Ops, SparseCore 0:
  224.5 60.9 all-reduce.33
  607.3 27.0 all-gather.1
where the time goes:
time: 780 us; the launch traced here: 770 us
  waiting for transfers between devices  319 us (41%)
  local copies, waits for them, and re-layouts  158 us (20%)
  blocking collectives  112 us (14%)
  other arithmetic  100 us (13%)
  starting transfers between devices  40.8 us (5%)
  matrix products  25.9 us (3%)
  between operations  14.3 us (2%)
    all_to_all x1, blocking collectives, body(): lax.all_to_all(adjoint, 'band', split_axis=2, concat_axis=1, tiled=True)  98.4 us
    all_to_all x1, waiting for transfers between devices, body(): lax.all_to_all(members, 'band', split_axis=1, concat_axis=2, tiled=True)  88.5 us
    all_to_all x1, waiting for transfers between devices, body(): lax.all_to_all(controls, 'band', split_axis=1, concat_axis=2, tiled=True)  82.4 us
    psum x1, waiting for transfers between devices, body(): summed = lax.psum(partial_value, 'member')  61.1 us
    all_to_all x1, waiting for transfers between devices, body(): lax.all_to_all(summed, 'band', split_axis=1, concat_axis=0, tiled=True)  46.9 us
    concatenate x3, other arithmetic, with_halo(): value = jnp.concatenate([before, value, after], axis=dim)  35.3 us
    all_gather x1, waiting for transfers between devices, body(): lax.all_gather(level_grad, 'member', axis=2, tiled=True)[None]  27.2 us
    unnamed x18, local copies, waits for them, and re-layouts  23.1 us
  transfers between devices with their start and end apart: 19, of which 12 were waited for; matrix products, arithmetic and copies ran while one was open for 8% of the time, Pallas kernels for 0%

commit v1 on v0

--- a/solution.py
+++ b/solution.py
@@ -75,7 +75,13 @@
     rowwise = jnp.einsum("klyx,ux->klyu", level_ctrl, loc_lon, precision=highest)
     fields = jnp.einsum("vy,klyx->klvx", loc_lat, rowwise, precision=highest)
     partial_value = jnp.sum(level_members * fields, axis=0) * member_scale
-    summed = lax.psum(partial_value, "member")
+    devices = lax.axis_size("member")
+    summed, far = (partial_value, 1)
+    while far < devices:
+        summed = summed + lax.ppermute(
+            summed, "member", [(i_2, i_2 ^ far) for i_2 in range(devices)]
+        )
+        far = 2 * far
     summed = lax.all_to_all(summed, "band", split_axis=1, concat_axis=0, tiled=True)
     wrapped = jnp.concatenate([summed[:, :, -2:], summed, summed[:, :, :2]], axis=2)
     extended = lax.dynamic_slice_in_dim(

time: 780 us -> 814 us (1.044)
  waiting for transfers between devices: 319 us -> 355 us
    ppermute x0 -> x3, waiting for transfers between devices: none -> 95.5 us  [body(): lax.ppermute(summed, 'member', [(i_2, i_2 ^ far) for i_2 in range(devices)])]
    psum x1 -> x0, waiting for transfers between devices: 61.1 us -> none  [body(): summed = lax.psum(partial_value, 'member')]
  transfers between devices with their start and end apart: 19 -> 21, of which waited for: 12 -> 15; matrix products, arithmetic and copies ran while one was open for 8% -> 8% of each run, Pallas kernels for 0% -> 0%
where the time goes in v1:
time: 814 us; the launch traced here: 804 us
  waiting for transfers between devices  355 us (44%)
  local copies, waits for them, and re-layouts  157 us (19%)
  blocking collectives  113 us (14%)
  other arithmetic  99.8 us (12%)
  starting transfers between devices  38.9 us (5%)
  matrix products  25.9 us (3%)
  between operations  14.3 us (2%)
    all_to_all x1, blocking collectives, body(): lax.all_to_all(adjoint, 'band', split_axis=2, concat_axis=1, tiled=True)  98.4 us
    ppermute x3, waiting for transfers between devices, body(): lax.ppermute(summed, 'member', [(i_2, i_2 ^ far) for i_2 in range(devices)])  95.5 us
    all_to_all x1, waiting for transfers between devices, body(): lax.all_to_all(members, 'band', split_axis=1, concat_axis=2, tiled=True)  88.5 us
    all_to_all x1, waiting for transfers between devices, body(): lax.all_to_all(controls, 'band', split_axis=1, concat_axis=2, tiled=True)  82.4 us
    all_to_all x1, waiting for transfers between devices, body(): lax.all_to_all(summed, 'band', split_axis=1, concat_axis=0, tiled=True)  47 us
    concatenate x3, other arithmetic, with_halo(): value = jnp.concatenate([before, value, after], axis=dim)  35.3 us
    all_gather x1, waiting for transfers between devices, body(): lax.all_gather(level_grad, 'member', axis=2, tiled=True)[None]  27.2 us
    unnamed x18, local copies, waits for them, and re-layouts  23.4 us
  transfers between devices with their start and end apart: 21, of which 15 were waited for; matrix products, arithmetic and copies ran while one was open for 8% of the time, Pallas kernels for 0%

profile of v1, /device:TPU:0, one launch (start us, length us, event | category | flops | bytes accessed | tf_op | source)
XLA Modules:
  0.0 803.8 jit_solution(13347105874040606656)
XLA Ops:
  6.5 5.0 copy.99
  11.5 6.3 all-to-all-start
  17.9 4.9 copy.103
  22.8 88.5 %all-to-all-done = f32[2,16,64,512]{3,2,0,1:T(8,128)} async-done(((f32[2,16,64,512]{3,2,0,1:T(8,128)}), f32[2,16,64,512]{3,2,0,1:T(8,128)}, u32[]{:S(2)}, u32[]{:S(2)}) %all-to-all-start) | async-done | bytes 4194336 | tf_op jit(solution)/shard_map/all_to_all | solution.py:73
  111.3 4.9 all-to-all-start.1
  116.2 4.9 copy.101
  121.1 5.3 copy.107
  126.4 82.4 %all-to-all-done.1 = f32[2,16,64,512]{3,2,0,1:T(8,128)} async-done(((f32[2,16,64,512]{3,2,0,1:T(8,128)}), f32[2,16,64,512]{3,2,0,1:T(8,128)}, u32[]{:S(2)}, u32[]{:S(2)}) %all-to-all-start.1) | async-done | bytes 4194336 | tf_op jit(solution)/shard_map/all_to_all | solution.py:72
  208.8 2.8 copy.105
  211.6 7.2 fusion.20
  218.8 4.1 fusion.10
  223.1 4.1 collective-permute-done
  227.5 1.6 collective-permute-start.1
  229.2 46.1 %collective-permute-done.1 = f32[4,256,512]{1,2,0:T(8,128)S(1)} collective-permute-done((f32[4,256,512]{1,2,0:T(8,128)S(1)}, f32[4,256,512]{1,2,0:T(8,128)S(1)}, u32[]{:S(2)}, u32[]{:S(2)}) %collective-permute-start.1) | collective-permute-done | bytes 2097184 | tf_op jit(solution)/shard_map/ppermute | solution.py:81
  275.6 1.7 collective-permute-start.2
  277.2 45.2 %collective-permute-done.2 = f32[4,256,512]{1,2,0:T(8,128)S(1)} collective-permute-done((f32[4,256,512]{1,2,0:T(8,128)S(1)}, f32[4,256,512]{1,2,0:T(8,128)S(1)}, u32[]{:S(2)}, u32[]{:S(2)}) %collective-permute-start.2) | collective-permute-done | bytes 2097184 | tf_op jit(solution)/shard_map/ppermute | solution.py:81
  322.7 2.2 copy.108
  324.9 3.6 all-to-all-start.2
  328.5 47.0 %all-to-all-done.2 = f32[4,256,512]{2,0,1:T(4,128)S(1)} async-done(((f32[4,256,512]{2,0,1:T(4,128)}), f32[4,256,512]{2,0,1:T(4,128)S(1)}, u32[]{:S(2)}, u32[]{:S(2)}) %all-to-all-start.2) | async-done | bytes 2097184 | tf_op jit(solution)/shard_map/all_to_all | solution.py:85
  379.9 4.2 collective-permute-done.4
  386.4 2.3 add_bitcast_fusion.3
  388.7 3.7 pad_maximum_fusion.2
  392.4 8.6 %copy.114 = f32[16,256,64,4]{1,0,3,2:T(8,128)} copy(f32[16,256,64,4]{2,0,1,3:T(8,128)} %pad_maximum_fusion.2) | data formatting | bytes 8388608 | tf_op jit(solution)/shard_map/stack | solution.py:56
  403.3 2.7 collective-permute-done.6
  406.0 2.6 pad_maximum_fusion.3
  408.6 2.1 fusion.42
  410.7 2.6 copy.118
  415.7 4.5 collective-permute-start.8
  425.2 5.8 copy.123
  431.0 5.6 copy.124
  437.9 1.4 copy.119
  439.3 2.6 copy.122
  441.9 20.1 %fusion.3 = f32[16,256,256]{1,0,2:T(8,128)} fusion(f32[16,256,256]{1,0,2:T(8,128)} %copy.124, f32[16,256,256]{1,0,2:T(8,128)} %copy.123, f32[16,1,258]{1,0,2:T(8,128)} %copy.122, f32[16,256,1]{1,0,2:T(8,128)S(1)} %collective-permute-done.5, f32[16,256,256]{1,0,2:T(8,128)} %bitcast.240, f32[16,256,1]{1,0,2:T(8,128)S(1)} %collective-permute-done.6, ...), kind=kLoop, calls=%fused_computation.17 | loop fusion | flops 19922944 | bytes 18153728 | tf_op jit(solution)/shard_map/mul | solution.py:101
  462.0 10.8 %broadcast_multiply_fusion = f32[4,16,256,256]{2,1,3,0:T(8,128)} fusion(f32[16,256,256]{1,0,2:T(8,128)} %fusion.3, f32[4,256,256]{1,2,0:T(8,128)} %copy.125), kind=kLoop, calls=%fused_computation.3 | loop fusion | flops 4194304 | bytes 22020096 | tf_op jit(solution)/shard_map/mul | solution.py:102
  474.3 2.0 collective-permute-done.10
  476.2 2.2 collective-permute-done.9
  478.4 6.8 pad_maximum_fusion.1
  485.3 7.3 fusion.40
  492.6 6.5 copy.126
  499.1 2.9 collective-permute-start.11
  502.0 6.5 copy.127
  509.8 6.6 copy.128
  516.4 6.3 copy.129
  522.7 25.9 %pad_maximum_fusion = f32[4,16,258,258]{2,1,3,0:T(8,128)} fusion(f32[4,16,1,258]{2,1,3,0:T(8,128)} %copy.129, f32[4,16,256,1]{2,1,3,0:T(8,128)S(1)} %collective-permute-done.10, f32[4,16,256,256]{2,1,3,0:T(8,128)} %broadcast_multiply_fusion, f32[4,16,256,1]{2,1,3,0:T(8,128)S(1)} %collective-permute-done.9, f32[4,16,1,258]{2,1,3,0:T(8,128)} %copy.128), kind=kLoop, calls=%fused_computation | loop fusion | flops 17040384 | bytes 34080768 | tf_op jit(solution)/shard_map/concatenate | solution.py:20
  548.6 17.6 %slice_bitcast_fusion.3 = (f32[16,258,258]{1,0,2:T(8,128)}, f32[16,258,258]{1,0,2:T(8,128)}, f32[16,258,258]{1,0,2:T(8,128)}, f32[16,258,258]{1,0,2:T(8,128)}) fusion(f32[4,16,258,258]{2,1,3,0:T(8,128)} %pad_maximum_fusion), kind=kLoop, calls=%fused_computation.7 | loop fusion | bytes 34080768 | tf_op jit(solution)/shard_map/squeeze | solution.py:107
  566.2 9.4 %slice_add_fusion = f32[16,256,256]{1,0,2:T(8,128)S(1)} fusion(f32[16,258,258]{1,0,2:T(8,128)} %get-tuple-element.56, f32[16,258,258]{1,0,2:T(8,128)} %get-tuple-element.57, f32[16,258,258]{1,0,2:T(8,128)} %get-tuple-element.58, f32[16,258,258]{1,0,2:T(8,128)} %get-tuple-element.55, f32[16,256,256]{1,0,2:T(8,128)S(1)} %copy-done.1, f32[256,256]{0,1:T(8,128)S(1)} %copy.102), kind=kLoop, calls=%fused_computation.9 | loop fusion | flops 5242880 | bytes 25427968 | tf_op jit(solution)/shard_map/add | solution.py:106
  575.6 3.0 fusion.17
  578.7 1.6 multiply_bitcast_fusion.9
  580.2 5.0 pad_add_fusion
  585.2 2.2 copy.139
  591.5 15.6 %scatter-add.14 = f32[16,68,64]{2,0,1:T(8,128)S(1)} dynamic-update-slice(f32[16,68,64]{2,0,1:T(8,128)S(1)} %slice.339, f32[16,68,2]{2,0,1:T(8,128)S(1)} %slice_add_fusion.4, s32[]{:T(128)} %constant.132.clone.1, s32[]{:T(128)} %constant.132.clone.1, s32[]{:T(128)} %constant.145.clone.1) | dynamic-update-slice | bytes 17412 | tf_op jit(solution)/shard_map/scatter-add | solution.py:117
  607.8 7.0 scatter-add.15
  616.2 5.2 collective-permute-start.16
  621.4 1.4 collective-permute-done.16
  623.3 14.3 %all_to_all.90 = f32[4,1,16384]{2,1,0:T(1,128)S(1)} all-to-all(f32[4,1,16384]{2,1,0:T(1,128)S(1)} %reshape.202), channel_id=1, replica_groups=mesh['member'=8,'band'=4] {'band'}, dimensions={0} | all-to-all | bytes 524288 | tf_op jit(solution)/shard_map/all_to_all | solution.py:124
  641.1 27.2 %all-gather.2.cloned.1.call-done = f32[4,256,512]{1,2,0:T(8,128)} async-done(((f32[4,256,64]{1,2,0:T(8,128)}), f32[4,256,512]{1,2,0:T(8,128)}) %all-gather.2.cloned.1.call-update) | async-done | bytes 2097168 | tf_op jit(solution)/shard_map/all_gather | solution.py:127
  668.3 1.9 copy.154
  670.2 9.8 %fusion.11 = f32[2,4,256,512]{2,3,1,0:T(8,128)S(1)} fusion(f32[2,4,256,512]{3,2,1,0:T(8,128)} %bitcast.242, f32[4,256,512]{2,1,0:T(8,128)S(1)} %copy.154, f32[512,512]{1,0:T(8,128)S(1)} %copy-done), kind=kOutput, calls=%fused_computation.33 | convolution fusion | flops 6444548096 | bytes 11534336 | tf_op jit(solution)/shard_map/klyu,ux->klyx/dot_general | solution.py:130
  680.0 4.9 convolution_bitcast_fusion
  685.0 5.5 copy.156
  690.4 98.4 %all_to_all.91 = f32[2,4,256,512]{3,1,0,2:T(4,128)S(1)} all-to-all(f32[2,4,256,512]{3,1,0,2:T(4,128)} %copy.156), channel_id=1, replica_groups=mesh['member'=8,'band'=4] {'band'}, dimensions={2} | all-to-all | bytes 8388608 | tf_op jit(solution)/shard_map/all_to_all | solution.py:132
  788.8 2.4 copy.157
  792.0 1.5 copy-done.2
  793.5 3.0 add.243
  (83 shorter events, 32.1 us)
Async XLA Ops:
  6.5 205.0 %copy-start = (f32[512,512]{1,0:T(8,128)S(1)}, f32[512,512]{1,0:T(8,128)}, u32[]{:S(2)}) copy-start(f32[512,512]{1,0:T(8,128)} %param.17) | copy-start | bytes 3145732
  11.5 99.8 %all-to-all-start = ((f32[2,16,64,512]{3,2,0,1:T(8,128)}), f32[2,16,64,512]{3,2,0,1:T(8,128)}, u32[]{:S(2)}, u32[]{:S(2)}) async-start(f32[2,16,64,512]{3,2,0,1:T(8,128)} %copy.99), calls=%async_computation | async-start | bytes 8388608 | tf_op jit(solution)/shard_map/all_to_all | solution.py:73
  111.3 97.5 %all-to-all-start.1 = ((f32[2,16,64,512]{3,2,0,1:T(8,128)}), f32[2,16,64,512]{3,2,0,1:T(8,128)}, u32[]{:S(2)}, u32[]{:S(2)}) async-start(f32[2,16,64,512]{3,2,0,1:T(8,128)} %copy.103), calls=%async_computation.1 | async-start | bytes 8388608 | tf_op jit(solution)/shard_map/all_to_all | solution.py:72
  211.6 7.2 copy-start.3
  211.6 7.2 copy-start.4
  223.0 4.2 collective-permute-start
  227.5 47.7 %collective-permute-start.1 = (f32[4,256,512]{1,2,0:T(8,128)S(1)}, f32[4,256,512]{1,2,0:T(8,128)S(1)}, u32[]{:S(2)}, u32[]{:S(2)}) collective-permute-start(f32[4,256,512]{1,2,0:T(8,128)S(1)} %fusion.38), channel_id=1, source_target_pairs={{0,8},{4,12},{8,0},{12,4},{16,24},{20,28},{24,16},{28,20},{1,9},{5... | collective-permute-start | bytes 6291464 | tf_op jit(solution)/shard_map/ppermute | solution.py:81
  275.6 46.9 %collective-permute-start.2 = (f32[4,256,512]{1,2,0:T(8,128)S(1)}, f32[4,256,512]{1,2,0:T(8,128)S(1)}, u32[]{:S(2)}, u32[]{:S(2)}) collective-permute-start(f32[4,256,512]{1,2,0:T(8,128)S(1)} %add.204), channel_id=1, source_target_pairs={{0,16},{4,20},{8,24},{12,28},{16,0},{20,4},{24,8},{28,12},{1,17},{... | collective-permute-start | bytes 6291464 | tf_op jit(solution)/shard_map/ppermute | solution.py:81
  324.9 50.6 %all-to-all-start.2 = ((f32[4,256,512]{2,0,1:T(4,128)}), f32[4,256,512]{2,0,1:T(4,128)S(1)}, u32[]{:S(2)}, u32[]{:S(2)}) async-start(f32[4,256,512]{2,0,1:T(4,128)} %copy.108), calls=%async_computation.2 | async-start | bytes 4194304 | tf_op jit(solution)/shard_map/all_to_all | solution.py:85
  328.5 339.8 %all-gather.2.cloned.1.call-start = ((), (), s32[]{:S(2)}) async-start(), calls=%async_computation.5 | async-start | bytes 2359296 | tf_op jit(solution)/shard_map/all_gather | solution.py:127
  377.1 2.7 collective-permute-start.3
  378.4 5.6 collective-permute-start.4
  401.7 1.5 collective-permute-start.5
  401.8 4.2 collective-permute-start.6
  413.3 24.6 %collective-permute-start.7 = (f32[16,1,258]{2,0,1:T(8,128)S(1)}, f32[16,1,258]{2,0,1:T(8,128)S(1)}, u32[]{:S(2)}, u32[]{:S(2)}) collective-permute-start(f32[16,1,258]{2,0,1:T(8,128)S(1)} %copy.118), channel_id=1, source_target_pairs={{1,0},{2,1},{3,2},{5,4},{6,5},{7,6},{9,8},{10,9},{11,10},{13,12},{... | collective-permute-start | bytes 49544 | tf_op jit(solution)/shard_map/ppermute | solution.py:19
  415.7 23.6 %collective-permute-start.8 = (f32[16,1,258]{2,0,1:T(8,128)S(1)}, f32[16,1,258]{2,0,1:T(8,128)S(1)}, u32[]{:S(2)}, u32[]{:S(2)}) collective-permute-start(f32[16,1,258]{2,0,1:T(8,128)S(1)} %copy.121), channel_id=1, source_target_pairs={{0,1},{1,2},{2,3},{4,5},{5,6},{6,7},{8,9},{9,10},{10,11},{12,13},{... | collective-permute-start | bytes 49544 | tf_op jit(solution)/shard_map/ppermute | solution.py:18
  431.0 5.6 slice-start
  473.7 2.5 collective-permute-start.10
  473.8 4.6 collective-permute-start.9
  499.1 10.7 %collective-permute-start.11 = (f32[4,16,1,258]{3,1,2,0:T(8,128)S(1)}, f32[4,16,1,258]{3,1,2,0:T(8,128)S(1)}, u32[]{:S(2)}, u32[]{:S(2)}) collective-permute-start(f32[4,16,1,258]{3,1,2,0:T(8,128)S(1)} %copy.126), channel_id=1, source_target_pairs={{0,1},{1,2},{2,3},{4,5},{5,6},{6,7},{8,9},{9,10},{10,11},{12,13},{... | collective-permute-start | bytes 198152 | tf_op jit(solution)/shard_map/ppermute | solution.py:18
  508.5 7.9 collective-permute-start.12
  548.6 17.6 %copy-start.1 = (f32[16,256,256]{1,0,2:T(8,128)S(1)}, f32[16,256,256]{1,0,2:T(8,128)}, u32[]{:S(2)}) copy-start(f32[16,256,256]{1,0,2:T(8,128)} %fusion.3) | copy-start | bytes 12582916
  589.3 1.7 collective-permute-start.13
  590.0 17.4 %collective-permute-start.14 = (f32[16,68,2]{1,0,2:T(8,128)S(1)}, f32[16,68,2]{1,0,2:T(8,128)S(1)}, u32[]{:S(2)}, u32[]{:S(2)}) collective-permute-start(f32[16,68,2]{1,0,2:T(8,128)S(1)} %copy.149), channel_id=1, source_target_pairs={{0,4},{4,8},{8,12},{12,16},{16,20},{20,24},{24,28},{28,0},{1,5},{5... | collective-permute-start | bytes 26120 | tf_op jit(solution)/shard_map/ppermute | solution.py:26
  614.9 6.5 collective-permute-start.15
  616.2 6.6 collective-permute-start.16
  670.2 9.8 %copy-start.5 = (f32[256,256]{1,0:T(8,128)S(1)}, f32[256,256]{1,0:T(8,128)}, u32[]{:S(2)}) copy-start(f32[256,256]{1,0:T(8,128)} %param.18) | copy-start | bytes 786436
  791.3 2.2 copy-start.2
Sparse Core Ops, SparseCore 0:
  641.2 27.0 all-gather.1
